TPU v7x, 256 devices: a whole 4x4x8 slice. The times are simulated.
256 devices in a mesh: expert: 32 (over z, y), etp: 8 (over x, core).
Axes of the slice: x: 4, y: 4, z: 8, core: 2. Of those that a mesh axis runs over, the one named last changes fastest.
Arguments:
- tokens: bfloat16 [32768, 2560], P(('expert', 'etp')), may hold values from -6 to 6
- grad_out: bfloat16 [32768, 2560], P(('expert', 'etp')), may hold values from -6 to 6
- router_weight: bfloat16 [2560, 32], replicated, may hold values from -0.125 to 0.125
- expert_choice: int32 [32768, 1], P(('expert', 'etp')), may hold values from 0 to 31; in each aligned block of 128 rows (0 to 127, 128 to 255, ...) at most 6 rows name the same one
- gate_pre: bfloat16 [32, 1536, 4096], P('expert', None, 'etp'), may hold values from -6 to 6
- up_pre: bfloat16 [32, 1536, 4096], P('expert', None, 'etp'), may hold values from -6 to 6
- w_gate: bfloat16 [32, 2560, 4096], P('expert', None, 'etp'), may hold values from -0.125 to 0.125
- w_up: bfloat16 [32, 2560, 4096], P('expert', None, 'etp'), may hold values from -0.125 to 0.125
- w_down: bfloat16 [32, 4096, 2560], P('expert', 'etp'), may hold values from -0.09375 to 0.09375
Outputs:
- token_grad: bfloat16 [32768, 2560], P(('expert', 'etp'))
- router_grad: float32 [2560, 32], replicated
Inputs may be any that keep to these rules, and one draw needn't show every extreme that they name: `expert_choice`: within the 128 tokens of one device no expert is chosen more than 6 times, and in every draw some expert is chosen exactly 6 times by the tokens of some device.
All inputs are finite; a program needn't handle non-finite values.
Results may differ from a plain program's by a relative error of at most 0.015.
Values may be sent and summed in bfloat16 or wider, within the bound.
No kernel may reach another device: no remote copies, remote signals or barrier semaphores. Data moves between devices by JAX's collectives and lax.ppermute only.
A program may use at most 128 MiB of HBM per device.

v0:
```python
import jax
import jax.numpy as jnp
from jax import lax
from jax.sharding import PartitionSpec as P


def local(tokens, grad_out, router_weight, expert_choice, gate_pre, up_pre, w_gate, w_up, w_down):
    width = tokens.shape[1]
    experts = router_weight.shape[1]
    n_expert = lax.axis_size("expert")
    n_etp = lax.axis_size("etp")
    capacity = gate_pre.shape[1] // (n_expert * n_etp)
    contract = (((1,), (1,)), ((), ()))
    chosen_ids = expert_choice[:, 0]
    picked = chosen_ids[:, None] == jnp.arange(experts, dtype=jnp.int32)[None, :]
    logits = jnp.dot(tokens, router_weight, preferred_element_type=jnp.float32)
    score = jax.nn.sigmoid(jnp.sum(jnp.where(picked, logits, 0.0), axis=1))
    counts = picked.astype(jnp.int32)
    earlier = jnp.cumsum(counts, axis=0) - counts
    position = jnp.sum(earlier * counts, axis=1)
    target = chosen_ids * capacity + position
    placed = jnp.arange(experts * capacity, dtype=jnp.int32)[:, None] == target[None, :]
    onehot = placed.astype(jnp.bfloat16)
    outgoing = jnp.dot(onehot, grad_out, preferred_element_type=jnp.float32).astype(jnp.bfloat16)
    own = lax.all_to_all(outgoing, "expert", split_axis=0, concat_axis=0, tiled=True)
    arrived = lax.all_gather(own, "etp", axis=0, tiled=True)
    d_hidden = lax.dot_general(arrived, w_down[0], contract, preferred_element_type=jnp.float32)
    gate_f = gate_pre[0].astype(jnp.float32)
    up_f = up_pre[0].astype(jnp.float32)
    sig = jax.nn.sigmoid(gate_f)
    d_gate = (d_hidden * up_f * sig * (1.0 + gate_f * (1.0 - sig))).astype(jnp.bfloat16)
    d_up = (d_hidden * gate_f * sig).astype(jnp.bfloat16)
    terms = (
        lax.dot_general(d_gate, w_gate[0], contract, preferred_element_type=jnp.float32)
        + lax.dot_general(d_up, w_up[0], contract, preferred_element_type=jnp.float32)
    ).astype(jnp.bfloat16)
    summed = lax.psum_scatter(terms, "etp", scatter_dimension=0, tiled=True)
    returned = lax.all_to_all(summed, "expert", split_axis=0, concat_axis=0, tiled=True)
    fetched = lax.dot_general(
        onehot, returned, (((0,), (0,)), ((), ())), preferred_element_type=jnp.float32
    )
    inputs = tokens.astype(jnp.float32)
    d_logit = jnp.sum(inputs * fetched, axis=1) * score * (1.0 - score)
    column = lax.dot_general(
        picked.astype(jnp.bfloat16), router_weight, contract, preferred_element_type=jnp.float32
    )
    token_grad = (score[:, None] * fetched + d_logit[:, None] * column).astype(jnp.bfloat16)
    weighted = jnp.where(picked, d_logit[:, None], 0.0)
    local_terms = lax.dot_general(
        weighted,
        inputs,
        (((0,), (0,)), ((), ())),
        precision=lax.Precision.HIGHEST,
        preferred_element_type=jnp.float32,
    )
    mine = lax.all_to_all(
        local_terms.reshape(n_etp, experts // n_etp, width),
        "etp",
        split_axis=0,
        concat_axis=0,
        tiled=True,
    )
    mine = jnp.sum(mine, axis=0)
    mine = lax.psum(mine, "expert")
    router_grad = lax.all_gather(mine, "etp", axis=0, tiled=True).T
    return (token_grad, router_grad)


def solution(mesh):
    placed = (
        P(("expert", "etp"), None),
        P(("expert", "etp"), None),
        P(),
        P(("expert", "etp"), None),
        P("expert", None, "etp"),
        P("expert", None, "etp"),
        P("expert", None, "etp"),
        P("expert", None, "etp"),
        P("expert", "etp", None),
    )
    return jax.shard_map(
        local,
        mesh=mesh,
        in_specs=placed,
        out_specs=(P(("expert", "etp"), None), P()),
        check_vma=False,
    )
```

profile of v0, /device:TPU:1, one launch (start us, length us, event | category | flops | bytes accessed | tf_op | source)
XLA Modules:
  0.0 423.1 jit_solution(13606596880845416231)
XLA Ops:
  7.2 0.0 copy-start
  7.2 0.0 all-gather.3.cloned.1.call-start
  7.2 0.8 fusion.29
  8.0 0.1 copy.15
  8.1 0.2 reduce_window_sum.11
  8.3 0.1 copy.16
  8.4 0.7 select_reduce_fusion
  9.1 0.7 multiply_add_fusion
  9.7 2.5 convolution_convert_fusion
  12.2 2.3 all_to_all.19
  14.4 46.0 %all_to_all.29 = bf16[32,6,2560]{2,1,0:T(8,128)(2,1)} all-to-all(bf16[32,6,2560]{2,1,0:T(8,128)(2,1)} %all_to_all.19), channel_id=1, replica_groups=mesh['expert'=32,'etp'=8] {'expert'}, dimensions={0} | all-to-all | bytes 1966080 | tf_op jit(solution)/shard_map/all_to_all | solution.py:25
  60.4 2.3 all_to_all.21
  62.7 0.0 all-gather.3.cloned.1.call-update
  62.7 0.0 reduce-scatter.2.cloned.1.call-start
  62.8 47.8 %all-gather.3.cloned.1.call-done = bf16[1536,2560]{1,0:T(8,128)(2,1)} async-done(((bf16[192,2560]{1,0:T(8,128)(2,1)}), bf16[1536,2560]{1,0:T(8,128)(2,1)}) %all-gather.3.cloned.1.call-update) | async-done | bytes 7864336 | tf_op jit(solution)/shard_map/all_gather | solution.py:26
  110.6 0.0 copy-start.4
  110.6 0.0 copy-start.5
  110.6 7.5 %fusion.14 = f32[1536,512]{1,0:T(8,128)S(1)} fusion(bf16[1536,2560]{1,0:T(8,128)(2,1)} %all-gather.3.cloned.1.call-done, bf16[1,512,2560]{2,1,0:T(8,128)(2,1)} %param.17), kind=kOutput, calls=%fused_computation.21 | convolution fusion | flops 4026531840 | bytes 13631488 | tf_op jit(solution)/shard_map/dot_general | solution.py:27
  118.1 0.0 copy-start.6
  118.1 1.7 copy-done.6
  119.8 0.0 copy-done
  119.8 0.0 copy-done.4
  119.8 0.0 copy-done.5
  119.8 9.8 %fusion.12 = f32[1536,2560]{1,0:T(8,128)} fusion(bf16[1,2560,512]{2,1,0:T(8,128)(2,1)S(1)} %copy-done, f32[1536,512]{1,0:T(8,128)S(1)} %fusion.14, bf16[1,1536,512]{2,1,0:T(8,128)(2,1)S(1)} %copy-done.4, bf16[1,1536,512]{2,1,0:T(8,128)(2,1)S(1)} %copy-done.5), kind=kOutput, calls=%fused_computation.19 | convolution fusion | flops 4035969024 | bytes 24641536 | tf_op jit(solution)/shard_map/dot_general | solution.py:34
  129.6 15.2 %add_convert_fusion = bf16[1536,2560]{1,0:T(8,128)(2,1)} fusion(f32[1536,2560]{1,0:T(8,128)} %fusion.12, bf16[1,2560,512]{2,1,0:T(8,128)(2,1)} %param.16, f32[1536,512]{1,0:T(8,128)} %copy-done.6, bf16[1,1536,512]{2,1,0:T(8,128)(2,1)} %param.13), kind=kOutput, calls=%fused_computation | convolution fusion | flops 4039901184 | bytes 30932992 | tf_op jit(solution)/shard_map/dot_general | solution.py:35
  144.9 0.0 reduce-scatter.2.cloned.1.call-update
  144.9 0.0 copy-start.1
  144.9 0.0 copy-start.2
  144.9 0.0 copy-start.3
  144.9 51.8 %reduce-scatter.2.cloned.1.call-done = bf16[192,2560]{1,0:T(8,128)(2,1)} async-done(((bf16[1536,2560]{1,0:T(8,128)(2,1)}), bf16[192,2560]{1,0:T(8,128)(2,1)}) %reduce-scatter.2.cloned.1.call-update) | async-done | bytes 983056 | tf_op jit(solution)/shard_map/reduce_scatter | solution.py:37
  196.8 2.3 all_to_all.22
  199.0 9.7 %all-to-all-start.1 = ((bf16[32,6,2560]{2,1,0:T(8,128)(2,1)}), bf16[32,6,2560]{2,1,0:T(8,128)(2,1)}, u32[]{:S(2)}, u32[]{:S(2)}) async-start(bf16[32,6,2560]{2,1,0:T(8,128)(2,1)} %all_to_all.22), calls=%async_computation.2 | async-start | bytes 2621440 | tf_op jit(solution)/shard_map/all_to_all | solution.py:38
  208.7 0.0 copy-done.1
  208.7 0.0 copy-done.2
  208.8 0.0 copy-done.3
  208.8 0.3 fusion.23
  209.1 30.4 %all-to-all-done.1 = bf16[32,6,2560]{2,1,0:T(8,128)(2,1)} async-done(((bf16[32,6,2560]{2,1,0:T(8,128)(2,1)}), bf16[32,6,2560]{2,1,0:T(8,128)(2,1)}, u32[]{:S(2)}, u32[]{:S(2)}) %all-to-all-start.1) | async-done | bytes 983072 | tf_op jit(solution)/shard_map/all_to_all | solution.py:38
  239.5 2.2 all_to_all.24
  241.7 2.7 multiply_reduce_fusion
  244.4 1.1 fusion.27
  245.5 1.8 reshape.36
  247.3 7.3 %all-to-all-start.2 = ((f32[8,4,2560]{2,1,0:T(4,128)}), f32[8,4,2560]{2,1,0:T(4,128)S(1)}, u32[]{:S(2)}, u32[]{:S(2)}) async-start(f32[8,4,2560]{2,1,0:T(4,128)} %reshape.36), calls=%async_computation.3 | async-start | bytes 655360 | tf_op jit(solution)/shard_map/all_to_all | solution.py:56
  254.6 2.5 fusion.1
  257.1 4.6 %all-to-all-done.2 = f32[8,4,2560]{2,1,0:T(4,128)S(1)} async-done(((f32[8,4,2560]{2,1,0:T(4,128)}), f32[8,4,2560]{2,1,0:T(4,128)S(1)}, u32[]{:S(2)}, u32[]{:S(2)}) %all-to-all-start.2) | async-done | bytes 327712 | tf_op jit(solution)/shard_map/all_to_all | solution.py:56
  261.7 0.1 reduce_sum.39
  261.8 112.4 %psum.7 = f32[4,2560]{1,0:T(4,128)S(1)} all-reduce(f32[4,2560]{1,0:T(4,128)S(1)} %reduce_sum.39), channel_id=1, replica_groups=mesh['expert'=32,'etp'=8] {'expert'}, use_global_device_ids=true, to_apply=%region_6.7 | all-reduce | flops 10240 | bytes 81920 | tf_op jit(solution)/shard_map/psum | solution.py:64
  374.2 41.3 %all-gather = f32[8,4,2560]{2,1,0:T(4,128)S(1)} all-gather(f32[1,4,2560]{2,1,0:T(4,128)S(1)} %bitcast.37), channel_id=1, replica_groups=mesh['expert'=32,'etp'=8] {'etp'}, dimensions={0}, use_global_device_ids=true | all-gather | bytes 368640 | tf_op jit(solution)/shard_map/all_gather | solution.py:65
  415.5 0.8 reshape.40
  (1 shorter events, 0.0 us)
Async XLA Ops:
  7.2 112.6 %copy-start = (bf16[1,2560,512]{2,1,0:T(8,128)(2,1)S(1)}, bf16[1,2560,512]{2,1,0:T(8,128)(2,1)}, u32[]{:S(2)}) copy-start(bf16[1,2560,512]{2,1,0:T(8,128)(2,1)} %param.15) | copy-start | bytes 7864324
  7.2 103.4 %all-gather.3.cloned.1.call-start = ((), (), s32[]{:S(2)}) async-start(), calls=%async_computation.4 | async-start | bytes 8847360 | tf_op jit(solution)/shard_map/all_gather | solution.py:26
  62.7 134.0 %reduce-scatter.2.cloned.1.call-start = ((), (), s32[]{:S(2)}) async-start(), calls=%async_computation.5 | async-start | bytes 8847360 | tf_op jit(solution)/shard_map/reduce_scatter | solution.py:37
  110.6 9.3 %copy-start.4 = (bf16[1,1536,512]{2,1,0:T(8,128)(2,1)S(1)}, bf16[1,1536,512]{2,1,0:T(8,128)(2,1)}, u32[]{:S(2)}) copy-start(bf16[1,1536,512]{2,1,0:T(8,128)(2,1)} %param.14) | copy-start | bytes 4718596
  110.6 9.3 %copy-start.5 = (bf16[1,1536,512]{2,1,0:T(8,128)(2,1)S(1)}, bf16[1,1536,512]{2,1,0:T(8,128)(2,1)}, u32[]{:S(2)}) copy-start(bf16[1,1536,512]{2,1,0:T(8,128)(2,1)} %param.13) | copy-start | bytes 4718596
  118.1 1.7 copy-start.6
  144.9 63.8 %copy-start.1 = (bf16[128,2560]{1,0:T(8,128)(2,1)S(1)}, bf16[128,2560]{1,0:T(8,128)(2,1)}, u32[]{:S(2)}) copy-start(bf16[128,2560]{1,0:T(8,128)(2,1)} %param.9) | copy-start | bytes 1966084
  144.9 63.8 %copy-start.2 = (bf16[2560,32]{0,1:T(8,128)(2,1)S(1)}, bf16[2560,32]{0,1:T(8,128)(2,1)}, u32[]{:S(2)}) copy-start(bf16[2560,32]{0,1:T(8,128)(2,1)} %param.11) | copy-start | bytes 491524
  144.9 63.8 %copy-start.3 = (s32[128,1]{0,1:T(1,128)S(1)}, s32[128,1]{0,1:T(1,128)}, u32[]{:S(2)}) copy-start(s32[128,1]{0,1:T(1,128)} %param.12) | copy-start | bytes 1540
  199.0 40.4 %all-to-all-start.1 = ((bf16[32,6,2560]{2,1,0:T(8,128)(2,1)}), bf16[32,6,2560]{2,1,0:T(8,128)(2,1)}, u32[]{:S(2)}, u32[]{:S(2)}) async-start(bf16[32,6,2560]{2,1,0:T(8,128)(2,1)} %all_to_all.22), calls=%async_computation.2 | async-start | bytes 2621440 | tf_op jit(solution)/shard_map/all_to_all | solution.py:38
  247.3 14.4 %all-to-all-start.2 = ((f32[8,4,2560]{2,1,0:T(4,128)}), f32[8,4,2560]{2,1,0:T(4,128)S(1)}, u32[]{:S(2)}, u32[]{:S(2)}) async-start(f32[8,4,2560]{2,1,0:T(4,128)} %reshape.36), calls=%async_computation.3 | async-start | bytes 655360 | tf_op jit(solution)/shard_map/all_to_all | solution.py:56
Sparse Core Ops, SparseCore 0:
  62.9 47.6 all-gather.2
  145.0 51.6 reduce-scatter.1
where the time goes:
time: 424 us; the launch traced here: 423 us
  blocking collectives  200 us (47%)
  waiting for transfers between devices  135 us (32%)
  matrix products  41.7 us (10%)
  starting transfers between devices  17.1 us (4%)
  between operations  14.1 us (3%)
  local copies, waits for them, and re-layouts  13.6 us (3%)
    psum x1, blocking collectives, local(): mine = lax.psum(mine, 'expert')  112 us
    reduce_scatter x1, waiting for transfers between devices, local(): summed = lax.psum_scatter(terms, 'etp', scatter_dimension=0, tiled=True)  51.8 us
    all_gather x1, waiting for transfers between devices, local(): arrived = lax.all_gather(own, 'etp', axis=0, tiled=True)  47.8 us
    all_to_all x1, blocking collectives, local(): lax.all_to_all(outgoing, 'expert', split_axis=0, concat_axis=0, tiled=True)  46 us
    all_gather x1, blocking collectives, local(): router_grad = lax.all_gather(mine, 'etp', axis=0, tiled=True).T  41.3 us
    all_to_all x1, waiting for transfers between devices, local(): lax.all_to_all(summed, 'expert', split_axis=0, concat_axis=0, tiled=True)  30.4 us
    dot_general x1, matrix products, local(): lax.dot_general(d_up, w_up[0], contract, preferred_element_type=jnp.float32)  15.2 us
    dot_general x1, matrix products, local(): lax.dot_general(d_gate, w_gate[0], contract, preferred_element_type=jnp.f...  9.81 us
  transfers between devices with their start and end apart: 4, of which 4 were waited for; matrix products, arithmetic and copies ran while one was open for 1% of the time, Pallas kernels for 0%

commit v1 on v0

--- a/solution.py
+++ b/solution.py
@@ -61,7 +61,9 @@
         tiled=True,
     )
     mine = jnp.sum(mine, axis=0)
-    mine = lax.psum(mine, "expert")
+    mine = mine
+    for hop in (1, 2, 4, 8, 16):
+        mine = mine + lax.ppermute(mine, "expert", [(dev, dev ^ hop) for dev in range(32)])
     router_grad = lax.all_gather(mine, "etp", axis=0, tiled=True).T
     return (token_grad, router_grad)
 

time: 424 us -> 311 us (0.73)
  blocking collectives: 200 us -> 80.9 us
    psum x1 -> x0, blocking collectives: 112 us -> none  [local(): mine = lax.psum(mine, 'expert')]
    all_gather x1, blocking collectives: 41.3 us -> 20.4 us  [local(): router_grad = lax.all_gather(mine, 'etp', axis=0, tiled=True).T]
    all_to_all x0 -> x1, blocking collectives: none -> 14.6 us  [local(): lax.all_to_all(local_terms.reshape(n_etp, experts // n_etp, width), 'etp'...]
    ppermute x0 -> x5, starting transfers between devices: none -> 10.1 us  [local(): lax.ppermute(mine, 'expert', [(dev, dev ^ hop) for dev in range(32)])]
    ppermute x0 -> x5, waiting for transfers between devices: none -> 8.71 us  [local(): lax.ppermute(mine, 'expert', [(dev, dev ^ hop) for dev in range(32)])]
    all_to_all x1 -> x0, starting transfers between devices: 7.3 us -> none  [local(): lax.all_to_all(local_terms.reshape(n_etp, experts // n_etp, width), 'etp'...]
    all_to_all x1 -> x0, waiting for transfers between devices: 4.58 us -> none  [local(): lax.all_to_all(local_terms.reshape(n_etp, experts // n_etp, width), 'etp'...]
  transfers between devices with their start and end apart: 4 -> 8, of which waited for: 4 -> 8; matrix products, arithmetic and copies ran while one was open for 1% -> 1% of each run, Pallas kernels for 0% -> 0%
where the time goes in v1:
time: 311 us
  waiting for transfers between devices  139 us (45%)
  blocking collectives  80.9 us (26%)
  matrix products  41.7 us (13%)
  starting transfers between devices  19.8 us (6%)
  between operations  14.2 us (5%)
  local copies, waits for them, and re-layouts  12.9 us (4%)
    reduce_scatter x1, waiting for transfers between devices, local(): summed = lax.psum_scatter(terms, 'etp', scatter_dimension=0, tiled=True)  51.8 us
    all_gather x1, waiting for transfers between devices, local(): arrived = lax.all_gather(own, 'etp', axis=0, tiled=True)  47.8 us
    all_to_all x1, blocking collectives, local(): lax.all_to_all(outgoing, 'expert', split_axis=0, concat_axis=0, tiled=True)  46 us
    all_to_all x1, waiting for transfers between devices, local(): lax.all_to_all(summed, 'expert', split_axis=0, concat_axis=0, tiled=True)  30.4 us
    all_gather x1, blocking collectives, local(): router_grad = lax.all_gather(mine, 'etp', axis=0, tiled=True).T  20.4 us
    dot_general x1, matrix products, local(): lax.dot_general(d_up, w_up[0], contract, preferred_element_type=jnp.float32)  15.3 us
    all_to_all x1, blocking collectives, local(): lax.all_to_all(local_terms.reshape(n_etp, experts // n_etp, width), 'etp'...  14.6 us
    ppermute x5, starting transfers between devices, local(): lax.ppermute(mine, 'expert', [(dev, dev ^ hop) for dev in range(32)])  10.1 us
  transfers between devices with their start and end apart: 8, of which 8 were waited for; matrix products, arithmetic and copies ran while one was open for 1% of the time, Pallas kernels for 0%

profile of v1, /device:TPU:1, one launch (start us, length us, event | category | flops | bytes accessed | tf_op | source)
XLA Modules:
  0.0 310.7 jit_solution(4350975677315968192)
XLA Ops:
  7.2 0.0 copy-start
  7.2 0.0 all-gather.3.cloned.1.call-start
  7.2 0.8 fusion.29
  8.0 0.1 copy.15
  8.1 0.2 reduce_window_sum.11
  8.3 0.1 copy.16
  8.4 0.7 select_reduce_fusion
  9.1 0.7 multiply_add_fusion
  9.7 2.5 convolution_convert_fusion
  12.2 2.3 all_to_all.19
  14.5 46.0 %all_to_all.29 = bf16[32,6,2560]{2,1,0:T(8,128)(2,1)} all-to-all(bf16[32,6,2560]{2,1,0:T(8,128)(2,1)} %all_to_all.19), channel_id=1, replica_groups=mesh['expert'=32,'etp'=8] {'expert'}, dimensions={0} | all-to-all | bytes 1966080 | tf_op jit(solution)/shard_map/all_to_all | solution.py:25
  60.4 2.3 all_to_all.21
  62.7 0.0 all-gather.3.cloned.1.call-update
  62.7 0.0 reduce-scatter.2.cloned.1.call-start
  62.8 47.8 %all-gather.3.cloned.1.call-done = bf16[1536,2560]{1,0:T(8,128)(2,1)} async-done(((bf16[192,2560]{1,0:T(8,128)(2,1)}), bf16[1536,2560]{1,0:T(8,128)(2,1)}) %all-gather.3.cloned.1.call-update) | async-done | bytes 7864336 | tf_op jit(solution)/shard_map/all_gather | solution.py:26
  110.6 0.0 copy-start.4
  110.6 0.0 copy-start.5
  110.6 7.5 %fusion.14 = f32[1536,512]{1,0:T(8,128)S(1)} fusion(bf16[1536,2560]{1,0:T(8,128)(2,1)} %all-gather.3.cloned.1.call-done, bf16[1,512,2560]{2,1,0:T(8,128)(2,1)} %param.17), kind=kOutput, calls=%fused_computation.21 | convolution fusion | flops 4026531840 | bytes 13631488 | tf_op jit(solution)/shard_map/dot_general | solution.py:27
  118.1 0.0 copy-start.6
  118.1 1.7 copy-done.6
  119.8 0.0 copy-done
  119.8 0.0 copy-done.4
  119.8 0.0 copy-done.5
  119.8 9.8 %fusion.12 = f32[1536,2560]{1,0:T(8,128)} fusion(bf16[1,2560,512]{2,1,0:T(8,128)(2,1)S(1)} %copy-done, f32[1536,512]{1,0:T(8,128)S(1)} %fusion.14, bf16[1,1536,512]{2,1,0:T(8,128)(2,1)S(1)} %copy-done.4, bf16[1,1536,512]{2,1,0:T(8,128)(2,1)S(1)} %copy-done.5), kind=kOutput, calls=%fused_computation.19 | convolution fusion | flops 4035969024 | bytes 24641536 | tf_op jit(solution)/shard_map/dot_general | solution.py:34
  129.7 15.3 %add_convert_fusion = bf16[1536,2560]{1,0:T(8,128)(2,1)} fusion(f32[1536,2560]{1,0:T(8,128)} %fusion.12, bf16[1,2560,512]{2,1,0:T(8,128)(2,1)} %param.16, f32[1536,512]{1,0:T(8,128)} %copy-done.6, bf16[1,1536,512]{2,1,0:T(8,128)(2,1)} %param.13), kind=kOutput, calls=%fused_computation | convolution fusion | flops 4039901184 | bytes 30932992 | tf_op jit(solution)/shard_map/dot_general | solution.py:35
  144.9 0.0 reduce-scatter.2.cloned.1.call-update
  144.9 0.0 copy-start.1
  144.9 0.0 copy-start.2
  145.0 0.0 copy-start.3
  145.0 51.8 %reduce-scatter.2.cloned.1.call-done = bf16[192,2560]{1,0:T(8,128)(2,1)} async-done(((bf16[1536,2560]{1,0:T(8,128)(2,1)}), bf16[192,2560]{1,0:T(8,128)(2,1)}) %reduce-scatter.2.cloned.1.call-update) | async-done | bytes 983056 | tf_op jit(solution)/shard_map/reduce_scatter | solution.py:37
  196.8 2.3 all_to_all.22
  199.0 9.7 %all-to-all-start.1 = ((bf16[32,6,2560]{2,1,0:T(8,128)(2,1)}), bf16[32,6,2560]{2,1,0:T(8,128)(2,1)}, u32[]{:S(2)}, u32[]{:S(2)}) async-start(bf16[32,6,2560]{2,1,0:T(8,128)(2,1)} %all_to_all.22), calls=%async_computation.2 | async-start | bytes 2621440 | tf_op jit(solution)/shard_map/all_to_all | solution.py:38
  208.7 0.0 copy-done.1
  208.7 0.0 copy-done.2
  208.8 0.0 copy-done.3
  208.8 0.3 fusion.23
  209.1 30.4 %all-to-all-done.1 = bf16[32,6,2560]{2,1,0:T(8,128)(2,1)} async-done(((bf16[32,6,2560]{2,1,0:T(8,128)(2,1)}), bf16[32,6,2560]{2,1,0:T(8,128)(2,1)}, u32[]{:S(2)}, u32[]{:S(2)}) %all-to-all-start.1) | async-done | bytes 983072 | tf_op jit(solution)/shard_map/all_to_all | solution.py:38
  239.5 2.3 all_to_all.24
  241.7 2.7 multiply_reduce_fusion
  244.4 1.1 fusion.27
  245.5 1.1 reshape.36
  246.6 14.6 %all_to_all.30 = f32[8,4,2560]{2,1,0:T(4,128)S(1)} all-to-all(f32[8,4,2560]{2,1,0:T(4,128)S(1)} %reshape.36), channel_id=1, replica_groups=mesh['expert'=32,'etp'=8] {'etp'}, dimensions={0} | all-to-all | bytes 655360 | tf_op jit(solution)/shard_map/all_to_all | solution.py:56
  261.2 0.1 reduce_sum.39
  261.2 1.3 collective-permute-start
  262.5 1.9 collective-permute-done
  264.4 2.8 collective-permute-start.1
  267.2 1.7 collective-permute-done.1
  268.8 1.0 collective-permute-start.2
  269.8 2.0 collective-permute-done.2
  271.8 2.4 collective-permute-start.3
  274.2 1.5 collective-permute-done.3
  275.7 2.6 collective-permute-start.4
  278.3 2.5 fusion.1
  280.9 1.7 collective-permute-done.4
  282.6 20.4 %all-gather = f32[8,4,2560]{2,1,0:T(4,128)S(1)} all-gather(f32[1,4,2560]{2,1,0:T(4,128)S(1)} %add_bitcast_fusion), channel_id=1, replica_groups=mesh['expert'=32,'etp'=8] {'etp'}, dimensions={0}, use_global_device_ids=true | all-gather | bytes 368640 | tf_op jit(solution)/shard_map/all_gather | solution.py:67
  303.0 0.8 reshape.40
  (6 shorter events, 0.1 us)
Async XLA Ops:
  7.2 112.7 %copy-start = (bf16[1,2560,512]{2,1,0:T(8,128)(2,1)S(1)}, bf16[1,2560,512]{2,1,0:T(8,128)(2,1)}, u32[]{:S(2)}) copy-start(bf16[1,2560,512]{2,1,0:T(8,128)(2,1)} %param.15) | copy-start | bytes 7864324
  7.2 103.4 %all-gather.3.cloned.1.call-start = ((), (), s32[]{:S(2)}) async-start(), calls=%async_computation.4 | async-start | bytes 8847360 | tf_op jit(solution)/shard_map/all_gather | solution.py:26
  62.7 134.1 %reduce-scatter.2.cloned.1.call-start = ((), (), s32[]{:S(2)}) async-start(), calls=%async_computation.5 | async-start | bytes 8847360 | tf_op jit(solution)/shard_map/reduce_scatter | solution.py:37
  110.6 9.3 %copy-start.4 = (bf16[1,1536,512]{2,1,0:T(8,128)(2,1)S(1)}, bf16[1,1536,512]{2,1,0:T(8,128)(2,1)}, u32[]{:S(2)}) copy-start(bf16[1,1536,512]{2,1,0:T(8,128)(2,1)} %param.14) | copy-start | bytes 4718596
  110.6 9.3 %copy-start.5 = (bf16[1,1536,512]{2,1,0:T(8,128)(2,1)S(1)}, bf16[1,1536,512]{2,1,0:T(8,128)(2,1)}, u32[]{:S(2)}) copy-start(bf16[1,1536,512]{2,1,0:T(8,128)(2,1)} %param.13) | copy-start | bytes 4718596
  118.1 1.7 copy-start.6
  144.9 63.8 %copy-start.1 = (bf16[128,2560]{1,0:T(8,128)(2,1)S(1)}, bf16[128,2560]{1,0:T(8,128)(2,1)}, u32[]{:S(2)}) copy-start(bf16[128,2560]{1,0:T(8,128)(2,1)} %param.9) | copy-start | bytes 1966084
  144.9 63.8 %copy-start.2 = (bf16[2560,32]{0,1:T(8,128)(2,1)S(1)}, bf16[2560,32]{0,1:T(8,128)(2,1)}, u32[]{:S(2)}) copy-start(bf16[2560,32]{0,1:T(8,128)(2,1)} %param.11) | copy-start | bytes 491524
  145.0 63.8 %copy-start.3 = (s32[128,1]{0,1:T(1,128)S(1)}, s32[128,1]{0,1:T(1,128)}, u32[]{:S(2)}) copy-start(s32[128,1]{0,1:T(1,128)} %param.12) | copy-start | bytes 1540
  199.0 40.4 %all-to-all-start.1 = ((bf16[32,6,2560]{2,1,0:T(8,128)(2,1)}), bf16[32,6,2560]{2,1,0:T(8,128)(2,1)}, u32[]{:S(2)}, u32[]{:S(2)}) async-start(bf16[32,6,2560]{2,1,0:T(8,128)(2,1)} %all_to_all.22), calls=%async_computation.2 | async-start | bytes 2621440 | tf_op jit(solution)/shard_map/all_to_all | solution.py:38
  261.2 3.1 %collective-permute-start = (f32[4,2560]{1,0:T(4,128)S(1)}, f32[4,2560]{1,0:T(4,128)S(1)}, u32[]{:S(2)}, u32[]{:S(2)}) collective-permute-start(f32[4,2560]{1,0:T(4,128)S(1)} %reduce_sum.39), channel_id=1, source_target_pairs={{0,8},{8,0},{16,24},{24,16},{32,40},{40,32},{48,56},{56,48},{64,72... | collective-permute-start | bytes 122888 | tf_op jit(solution)/shard_map/ppermute | solution.py:66
  264.4 4.4 %collective-permute-start.1 = (f32[4,2560]{1,0:T(4,128)S(1)}, f32[4,2560]{1,0:T(4,128)S(1)}, u32[]{:S(2)}, u32[]{:S(2)}) collective-permute-start(f32[4,2560]{1,0:T(4,128)S(1)} %add.52), channel_id=1, source_target_pairs={{0,16},{8,24},{16,0},{24,8},{32,48},{40,56},{48,32},{56,40},{64,80... | collective-permute-start | bytes 122888 | tf_op jit(solution)/shard_map/ppermute | solution.py:66
  268.8 2.9 collective-permute-start.2
  271.8 3.9 %collective-permute-start.3 = (f32[4,2560]{1,0:T(4,128)S(1)}, f32[4,2560]{1,0:T(4,128)S(1)}, u32[]{:S(2)}, u32[]{:S(2)}) collective-permute-start(f32[4,2560]{1,0:T(4,128)S(1)} %add.54), channel_id=1, source_target_pairs={{0,64},{8,72},{16,80},{24,88},{32,96},{40,104},{48,112},{56,120},{... | collective-permute-start | bytes 122888 | tf_op jit(solution)/shard_map/ppermute | solution.py:66
  275.7 6.9 %collective-permute-start.4 = (f32[4,2560]{1,0:T(4,128)S(1)}, f32[4,2560]{1,0:T(4,128)S(1)}, u32[]{:S(2)}, u32[]{:S(2)}) collective-permute-start(f32[4,2560]{1,0:T(4,128)S(1)} %add.55), channel_id=1, source_target_pairs={{0,128},{8,136},{16,144},{24,152},{32,160},{40,168},{48,176},{56,1... | collective-permute-start | bytes 122888 | tf_op jit(solution)/shard_map/ppermute | solution.py:66
Sparse Core Ops, SparseCore 0:
  62.9 47.6 all-gather.2
  145.0 51.6 reduce-scatter.1
